TPU v7x, 32 devices: a whole 2x2x4 slice. The times are simulated.
32 devices in a mesh: prow: 16 (over z, y, x), pcol: 2 (over core).
Axes of the slice: x: 2, y: 2, z: 4, core: 2. Of those that a mesh axis runs over, the one named last changes fastest.
Arguments:
- right_sides: float32 [32, 1, 4096], P(None, None, 'prow'), may hold values from -6 to 6
- factor: bfloat16 [1, 4096, 8, 512], P(None, 'prow', None, 'pcol'), as said below
- node_sizes: int32 [7], replicated, may hold values from 1 to 9, 16 in all
- row_blocks: int32 [7, 16], replicated, may hold values 0 or 1
Outputs:
- forward: float32 [32, 1, 4096], P(None, None, 'prow')
- solution: float32 [32, 8, 512], P(None, None, 'pcol')
Inputs may be any that keep to these rules, and one draw needn't show every extreme that they name: factor is zero above its diagonal; its diagonal lies between 0.5 and 1. `row_blocks`: flags of tiles that belong to no proper ancestor of the supernode are ignored.
All inputs are finite; a program needn't handle non-finite values.
Results may differ from a plain program's by a relative error of at most 0.0047.
Values may be sent and summed in bfloat16 or wider, within the bound.
A program may use at most 64 MiB of HBM per device.

v0:
```python
import jax
import jax.numpy as jnp
from jax import lax
from jax.sharding import PartitionSpec as P

LEVELS = 3


def tree_tables(node_sizes, row_blocks):
    node_count = node_sizes.shape[0]
    tile_count = row_blocks.shape[1]
    tile_ends = jnp.cumsum(node_sizes)
    tile_ids = jnp.arange(tile_count, dtype=jnp.int32)
    node_of = jnp.sum((tile_ends[None, :] <= tile_ids[:, None]).astype(jnp.int32), axis=1)
    heap_label = node_count - jnp.arange(node_count, dtype=jnp.int32)
    node_depth = jnp.zeros((node_count,), jnp.int32)
    for exponent in range(1, LEVELS):
        node_depth = node_depth + (heap_label >= 2**exponent).astype(jnp.int32)
    gap_depth = jnp.maximum(node_depth[None, :] - node_depth[:, None], 0)
    ancestor = (node_depth[:, None] < node_depth[None, :]) & (
        jnp.right_shift(heap_label[None, :], gap_depth) == heap_label[:, None]
    )
    return (node_of, node_depth, ancestor)


def lookup(source, indices, length):
    hits = indices[:, None] == jnp.arange(length, dtype=jnp.int32)[None, :]
    return jnp.sum(jnp.where(hits, source[None, :], 0), axis=1)


def rows_from_columns(factor, vector, weights):
    blocks = lax.dot_general(
        vector, factor, (((2,), (3,)), ((1,), (2,))), preferred_element_type=jnp.float32
    )
    return jnp.sum(weights.T[:, None, :, None] * blocks, axis=0)


def columns_from_rows(factor, vector, weights):
    blocks = lax.dot_general(
        vector, factor, (((2,), (1,)), ((1,), (0,))), preferred_element_type=jnp.float32
    )
    return jnp.sum(weights[:, None, :, None] * blocks, axis=0)


def to_columns(vector):
    row_count = lax.axis_size("prow")
    col_count = lax.axis_size("pcol")
    row_groups = row_count // col_count
    col_index = lax.axis_index("pcol")
    rhs_count, row_tiles, tile_rows = vector.shape
    collected = lax.all_gather(vector, "prow", axis=1, tiled=True)
    collected = collected.reshape(rhs_count, row_groups, col_count, row_tiles, tile_rows)
    picked = lax.dynamic_index_in_dim(collected, col_index, 2, keepdims=False)
    return jnp.transpose(picked, (0, 2, 1, 3)).reshape(rhs_count, row_tiles * row_groups, tile_rows)


def to_rows(vector):
    row_count = lax.axis_size("prow")
    col_count = lax.axis_size("pcol")
    row_groups = row_count // col_count
    row_index = lax.axis_index("prow")
    rhs_count, col_tiles, tile_rows = vector.shape
    shaped = vector.reshape(rhs_count, col_tiles // row_groups, row_groups, tile_rows)
    chosen = lax.dynamic_index_in_dim(shaped, row_index // col_count, 2, keepdims=False)
    collected = lax.all_gather(chosen, "pcol", axis=1, tiled=True)
    collected = collected.reshape(rhs_count, col_count, col_tiles // row_groups, tile_rows)
    return lax.dynamic_index_in_dim(collected, row_index % col_count, 1, keepdims=False)


def sum_rows(partial_value):
    return lax.psum(partial_value, "pcol")


def sum_cols(partial_value):
    return lax.psum(partial_value, "prow")


def shards(right_sides, factor, node_sizes, row_blocks):
    row_count = lax.axis_size("prow")
    col_count = lax.axis_size("pcol")
    row_index = lax.axis_index("prow")
    col_index = lax.axis_index("pcol")
    row_tiles = factor.shape[0]
    col_tiles = factor.shape[2]
    rhs_count = right_sides.shape[0]
    tile_rows = right_sides.shape[2]
    node_count = node_sizes.shape[0]
    tile_count = row_blocks.shape[1]
    node_of, node_depth, ancestor = tree_tables(node_sizes, row_blocks)
    mine_rows = jnp.arange(row_tiles, dtype=jnp.int32) * row_count + row_index
    mine_cols = jnp.arange(col_tiles, dtype=jnp.int32) * col_count + col_index
    owner_rows = lookup(node_of, mine_rows, tile_count)
    owner_cols = lookup(node_of, mine_cols, tile_count)
    depth_rows = lookup(node_depth, owner_rows, node_count)
    depth_cols = lookup(node_depth, owner_cols, node_count)
    node_ids = jnp.arange(node_count, dtype=jnp.int32)
    hits_rows = owner_rows[:, None] == node_ids[None, :]
    hits_cols = owner_cols[:, None] == node_ids[None, :]
    above = jnp.any(
        hits_rows[:, None, :, None] & ancestor[None, None, :, :] & hits_cols[None, :, None, :],
        axis=(2, 3),
    )
    tile_hits = mine_rows[:, None] == jnp.arange(tile_count, dtype=jnp.int32)[None, :]
    flagged = jnp.any(
        tile_hits[:, None, None, :]
        & hits_cols[None, :, :, None]
        & (row_blocks == 1)[None, None, :, :],
        axis=(2, 3),
    )
    diagonal = owner_rows[:, None] == owner_cols[None, :]
    linked = above & flagged
    correction = jnp.zeros(right_sides.shape, jnp.float32)
    forward = jnp.zeros(right_sides.shape, jnp.float32)
    forward_cols = jnp.zeros((rhs_count, col_tiles, tile_rows), jnp.float32)
    for height in range(LEVELS - 1, -1, -1):
        at_rows = depth_rows == height
        at_cols = depth_cols == height
        current = (right_sides - correction).astype(jnp.bfloat16)
        solve_weights = (diagonal & at_rows[:, None]).astype(jnp.float32)
        solved = sum_rows(rows_from_columns(factor, to_columns(current), solve_weights))
        forward = forward + solved
        solved_cols = to_columns(solved.astype(jnp.bfloat16))
        forward_cols = forward_cols + solved_cols.astype(jnp.float32)
        if height > 0:
            update_weights = (linked & at_cols[None, :]).astype(jnp.float32)
            correction = correction + sum_rows(
                rows_from_columns(factor, solved_cols, update_weights)
            )
    solution = jnp.zeros((rhs_count, col_tiles, tile_rows), jnp.float32)
    correction_cols = jnp.zeros((rhs_count, col_tiles, tile_rows), jnp.float32)
    for height in range(LEVELS):
        at_rows = depth_rows == height
        at_cols = depth_cols == height
        if height == 0:
            current = forward.astype(jnp.bfloat16)
        else:
            current = to_rows((forward_cols - correction_cols).astype(jnp.bfloat16))
        solve_weights = (diagonal & at_cols[None, :]).astype(jnp.float32)
        solved = sum_cols(columns_from_rows(factor, current, solve_weights))
        solution = solution + solved
        if height < LEVELS - 1:
            solved_rows = to_rows(solved.astype(jnp.bfloat16))
            update_weights = (linked & at_rows[:, None]).astype(jnp.float32)
            correction_cols = correction_cols + sum_cols(
                columns_from_rows(factor, solved_rows, update_weights)
            )
    return (forward, solution)


def solution(mesh):
    in_specs = (P(None, None, "prow"), P(None, "prow", None, "pcol"), P(), P())
    out_specs = (P(None, None, "prow"), P(None, None, "pcol"))
    return jax.shard_map(shards, mesh=mesh, in_specs=in_specs, out_specs=out_specs, check_vma=False)
```

profile of v0, /device:TPU:0, one launch (start us, length us, event | category | flops | bytes accessed | tf_op | source)
XLA Modules:
  0.0 793.3 jit_solution(14260200867232302940)
XLA Ops:
  7.3 0.9 reduce-window.8
  8.3 0.6 select_reduce_fusion.3
  8.9 0.6 iota_compare_fusion.3
  9.5 1.3 select_reduce_fusion.2
  12.1 0.2 select_reduce_fusion.1
  12.4 0.1 copy.64
  12.5 0.2 select_reduce_fusion
  12.8 0.1 and_reduce_fusion.1
  12.9 0.5 copy-done.4
  13.4 0.6 and_convert_fusion.4
  14.7 43.8 %all_gather.30 = bf16[32,16,256]{2,0,1:T(8,128)(2,1)S(1)} all-gather(bf16[32,1,256]{2,0,1:T(8,128)(2,1)S(1)} %copy.112), channel_id=1, replica_groups=mesh['prow'=16,'pcol'=2] {'prow'}, dimensions={1}, use_global_device_ids=true | all-gather | bytes 278528 | tf_op jit(solution)/shard_map/all_gather | solution.py:51
  58.5 0.2 and_reduce_fusion
  58.7 0.4 fusion
  59.2 3.4 psum.70
  62.6 36.9 %all_gather.31 = bf16[32,16,256]{2,0,1:T(8,128)(2,1)S(1)} all-gather(bf16[32,1,256]{2,0,1:T(8,128)(2,1)S(1)} %convert_element_type.179), channel_id=1, replica_groups=mesh['prow'=16,'pcol'=2] {'prow'}, dimensions={1}, use_global_device_ids=true | all-gather | bytes 278528 | tf_op jit(solution)/shard_map/all_gather | solution.py:51
  99.4 0.4 fusion.1
  99.9 3.4 psum.71
  103.3 38.9 %all_gather.32 = bf16[32,16,256]{2,0,1:T(8,128)(2,1)S(1)} all-gather(bf16[32,1,256]{2,0,1:T(8,128)(2,1)S(1)} %subtract_convert_fusion.2), channel_id=1, replica_groups=mesh['prow'=16,'pcol'=2] {'prow'}, dimensions={1}, use_global_device_ids=true | all-gather | bytes 278528 | tf_op jit(solution)/shard_map/all_gather | solution.py:51
  142.2 0.4 fusion.2
  142.6 3.4 psum.72
  146.1 36.9 %all_gather.33 = bf16[32,16,256]{2,0,1:T(8,128)(2,1)S(1)} all-gather(bf16[32,1,256]{2,0,1:T(8,128)(2,1)S(1)} %convert_element_type.183), channel_id=1, replica_groups=mesh['prow'=16,'pcol'=2] {'prow'}, dimensions={1}, use_global_device_ids=true | all-gather | bytes 278528 | tf_op jit(solution)/shard_map/all_gather | solution.py:51
  182.9 0.4 fusion.3
  183.4 3.4 psum.73
  186.8 39.0 %all_gather.34 = bf16[32,16,256]{2,0,1:T(8,128)(2,1)S(1)} all-gather(bf16[32,1,256]{2,0,1:T(8,128)(2,1)S(1)} %subtract_convert_fusion.1), channel_id=1, replica_groups=mesh['prow'=16,'pcol'=2] {'prow'}, dimensions={1}, use_global_device_ids=true | all-gather | bytes 278528 | tf_op jit(solution)/shard_map/all_gather | solution.py:51
  225.8 0.4 fusion.4
  226.2 3.4 psum.74
  229.6 1.0 convolution_multiply_fusion.4
  230.7 104.0 %all-reduce.6.cloned.1.call-done = f32[32,8,256]{2,0,1:T(8,128)} async-done(((f32[32,8,256]{2,0,1:T(8,128)}), f32[32,8,256]{2,0,1:T(8,128)}) %all-reduce.6.cloned.1.call-update) | async-done | bytes 262160 | tf_op jit(solution)/shard_map/psum | solution.py:75
  334.7 0.8 dynamic-slice_convert_fusion.1
  335.5 1.8 all_gather.36
  337.3 1.0 convolution_multiply_fusion.3
  338.3 40.2 %all_gather.35 = bf16[32,16,256]{2,0,1:T(8,128)(2,1)S(1)} all-gather(bf16[32,1,256]{2,0,1:T(8,128)(2,1)S(1)} %get-tuple-element.14), channel_id=1, replica_groups=mesh['prow'=16,'pcol'=2] {'prow'}, dimensions={1}, use_global_device_ids=true | all-gather | bytes 278528 | tf_op jit(solution)/shard_map/all_gather | solution.py:51
  378.6 68.9 %all-reduce.8.cloned.1.call-done = f32[32,8,256]{2,0,1:T(8,128)} async-done(((f32[32,8,256]{2,0,1:T(8,128)}), f32[32,8,256]{2,0,1:T(8,128)}) %all-reduce.8.cloned.1.call-update) | async-done | bytes 262160 | tf_op jit(solution)/shard_map/psum | solution.py:75
  447.5 0.8 subtract_convert_fusion
  448.3 1.8 all_gather.37
  450.1 1.0 convolution_multiply_fusion.2
  451.2 108.9 %all-reduce.10.cloned.1.call-done = f32[32,8,256]{2,0,1:T(8,128)} async-done(((f32[32,8,256]{2,0,1:T(8,128)}), f32[32,8,256]{2,0,1:T(8,128)}) %all-reduce.10.cloned.1.call-update) | async-done | bytes 262160 | tf_op jit(solution)/shard_map/psum | solution.py:75
  560.1 0.8 dynamic-slice_convert_fusion
  560.8 1.8 all_gather.38
  562.7 1.0 convolution_multiply_fusion.1
  563.7 108.7 %all-reduce.12.cloned.1.call-done = f32[32,8,256]{2,0,1:T(8,128)} async-done(((f32[32,8,256]{2,0,1:T(8,128)}), f32[32,8,256]{2,0,1:T(8,128)}) %all-reduce.12.cloned.1.call-update) | async-done | bytes 262160 | tf_op jit(solution)/shard_map/psum | solution.py:75
  672.5 0.8 fusion.16
  673.3 1.8 all_gather.39
  675.1 1.0 convolution_multiply_fusion
  676.1 0.6 copy.81
  676.8 108.1 %all-reduce.14.cloned.1.call-done = f32[32,8,256]{2,0,1:T(8,128)} async-done(((f32[32,8,256]{2,0,1:T(8,128)}), f32[32,8,256]{2,0,1:T(8,128)}) %all-reduce.14.cloned.1.call-update) | async-done | bytes 262160 | tf_op jit(solution)/shard_map/psum | solution.py:75
  784.9 1.0 add_add_fusion
  785.9 0.9 copy.82
  (35 shorter events, 0.7 us)
Async XLA Ops:
  7.2 51.5 %copy-start = (bf16[1,256,8,256]{3,2,1,0:T(8,128)(2,1)S(1)}, bf16[1,256,8,256]{3,2,1,0:T(8,128)(2,1)}, u32[]{:S(2)}) copy-start(bf16[1,256,8,256]{3,2,1,0:T(8,128)(2,1)} %param.5) | copy-start | bytes 3145732
  7.2 7.5 copy-start.3
  7.2 327.5 %all-reduce.6.cloned.1.call-start = ((), (), s32[]{:S(2)}) async-start(), calls=%async_computation | async-start | bytes 524288 | tf_op jit(solution)/shard_map/psum | solution.py:75
  12.7 0.7 copy-start.4
  230.6 216.9 %all-reduce.8.cloned.1.call-start = ((), (), s32[]{:S(2)}) async-start(), calls=%async_computation.1 | async-start | bytes 524288 | tf_op jit(solution)/shard_map/psum | solution.py:75
  338.3 221.8 %all-reduce.10.cloned.1.call-start = ((), (), s32[]{:S(2)}) async-start(), calls=%async_computation.2 | async-start | bytes 524288 | tf_op jit(solution)/shard_map/psum | solution.py:75
  451.1 221.4 %all-reduce.12.cloned.1.call-start = ((), (), s32[]{:S(2)}) async-start(), calls=%async_computation.3 | async-start | bytes 524288 | tf_op jit(solution)/shard_map/psum | solution.py:75
  563.7 221.2 %all-reduce.14.cloned.1.call-start = ((), (), s32[]{:S(2)}) async-start(), calls=%async_computation.4 | async-start | bytes 524288 | tf_op jit(solution)/shard_map/psum | solution.py:75
  675.1 109.8 %copy-start.2 = (f32[32,8,256]{2,0,1:T(8,128)S(1)}, f32[32,8,256]{2,0,1:T(8,128)}, u32[]{:S(2)}) copy-start(f32[32,8,256]{2,0,1:T(8,128)} %all-reduce.10.cloned.1.call-done) | copy-start | bytes 786436
  676.1 108.8 %copy-start.1 = (f32[32,8,256]{2,0,1:T(8,128)S(1)}, f32[32,8,256]{2,0,1:T(8,128)}, u32[]{:S(2)}) copy-start(f32[32,8,256]{2,0,1:T(8,128)} %all-reduce.6.cloned.1.call-done) | copy-start | bytes 786436
Sparse Core Ops, SparseCore 0:
  230.8 103.9 all-reduce.5
  340.5 106.9 all-reduce.7
  453.3 106.7 all-reduce.9
  565.7 106.6 all-reduce.11
  678.1 106.7 all-reduce.13
where the time goes:
time: 794 us; the launch traced here: 793 us
  waiting for transfers between devices  499 us (63%)
  blocking collectives  260 us (33%)
  between operations  16 us (2%)
    psum x5, waiting for transfers between devices, sum_cols(): return lax.psum(partial_value, 'prow')  499 us
    all_gather x6, blocking collectives, to_columns(): collected = lax.all_gather(vector, 'prow', axis=1, tiled=True)  236 us
    psum x5, blocking collectives, sum_rows(): return lax.psum(partial_value, 'pcol')  17 us
  transfers between devices with their start and end apart: 5, of which 5 were waited for; matrix products, arithmetic and copies ran while one was open for 0% of the time, Pallas kernels for 0%

commit v1 on v0

--- a/solution.py
+++ b/solution.py
@@ -72,7 +72,8 @@
 
 
 def sum_cols(partial_value):
-    return lax.psum(partial_value, "prow")
+    _proceed_lane = lambda tile_in: jnp.sum(lax.all_gather(tile_in, "prow"), axis=0)
+    return _proceed_lane(partial_value)
 
 
 def shards(right_sides, factor, node_sizes, row_blocks):

time: 794 us -> 638 us (0.80)
  waiting for transfers between devices: 499 us -> 332 us
  other arithmetic: 7.72 us -> 19.3 us
    psum x5 -> x0, waiting for transfers between devices: 499 us -> none  [sum_cols(): return lax.psum(partial_value, 'prow')]
    all_gather x0 -> x5, waiting for transfers between devices: none -> 332 us  [sum_cols(): lax.all_gather(tile_in, 'prow')]
    reduce_sum x0 -> x5, other arithmetic: none -> 12.5 us  [sum_cols(): jnp.sum(lax.all_gather(tile_in, 'prow'), axis=0)]
where the time goes in v1:
time: 638 us; the launch traced here: 637 us
  waiting for transfers between devices  332 us (52%)
  blocking collectives  260 us (41%)
  other arithmetic  19.3 us (3%)
  between operations  16 us (3%)
  matrix products  7.07 us (1%)
    all_gather x5, waiting for transfers between devices, sum_cols(): lax.all_gather(tile_in, 'prow')  332 us
    all_gather x6, blocking collectives, to_columns(): collected = lax.all_gather(vector, 'prow', axis=1, tiled=True)  235 us
    psum x5, blocking collectives, sum_rows(): return lax.psum(partial_value, 'pcol')  17 us
  transfers between devices with their start and end apart: 5, of which 5 were waited for; matrix products, arithmetic and copies ran while one was open for 0% of the time, Pallas kernels for 0%

profile of v1, /device:TPU:0, one launch (start us, length us, event | category | flops | bytes accessed | tf_op | source)
XLA Modules:
  0.0 636.8 jit_solution(6909736138122105296)
XLA Ops:
  7.3 0.9 reduce-window.8
  8.2 0.6 select_reduce_fusion.3
  8.9 1.3 select_reduce_fusion.2
  11.5 0.7 iota_compare_fusion.3
  12.8 0.2 select_reduce_fusion.1
  13.2 0.7 broadcast_compare_fusion
  13.8 0.2 select_reduce_fusion
  14.2 0.7 and_convert_fusion.4
  14.9 0.8 copy.111
  15.7 43.8 %all_gather.50 = bf16[32,16,256]{2,0,1:T(8,128)(2,1)S(1)} all-gather(bf16[32,1,256]{2,0,1:T(8,128)(2,1)S(1)} %copy.111), channel_id=1, replica_groups=mesh['prow'=16,'pcol'=2] {'prow'}, dimensions={1}, use_global_device_ids=true | all-gather | bytes 278528 | tf_op jit(solution)/shard_map/all_gather | solution.py:51
  59.4 0.2 and_reduce_fusion
  59.7 0.4 fusion
  60.1 3.4 psum.35
  63.5 36.9 %all_gather.51 = bf16[32,16,256]{2,0,1:T(8,128)(2,1)S(1)} all-gather(bf16[32,1,256]{2,0,1:T(8,128)(2,1)S(1)} %convert_element_type.179), channel_id=1, replica_groups=mesh['prow'=16,'pcol'=2] {'prow'}, dimensions={1}, use_global_device_ids=true | all-gather | bytes 278528 | tf_op jit(solution)/shard_map/all_gather | solution.py:51
  100.4 0.4 fusion.1
  100.8 3.4 psum.36
  104.2 0.8 subtract_convert_fusion.2
  105.0 38.9 %all_gather.52 = bf16[32,16,256]{2,0,1:T(8,128)(2,1)S(1)} all-gather(bf16[32,1,256]{2,0,1:T(8,128)(2,1)S(1)} %subtract_convert_fusion.2), channel_id=1, replica_groups=mesh['prow'=16,'pcol'=2] {'prow'}, dimensions={1}, use_global_device_ids=true | all-gather | bytes 278528 | tf_op jit(solution)/shard_map/all_gather | solution.py:51
  143.9 0.4 fusion.2
  144.3 3.4 psum.37
  147.8 36.9 %all_gather.53 = bf16[32,16,256]{2,0,1:T(8,128)(2,1)S(1)} all-gather(bf16[32,1,256]{2,0,1:T(8,128)(2,1)S(1)} %convert_element_type.183), channel_id=1, replica_groups=mesh['prow'=16,'pcol'=2] {'prow'}, dimensions={1}, use_global_device_ids=true | all-gather | bytes 278528 | tf_op jit(solution)/shard_map/all_gather | solution.py:51
  184.6 0.4 fusion.3
  185.1 3.4 psum.38
  188.5 39.0 %all_gather.54 = bf16[32,16,256]{2,0,1:T(8,128)(2,1)S(1)} all-gather(bf16[32,1,256]{2,0,1:T(8,128)(2,1)S(1)} %subtract_convert_fusion.1), channel_id=1, replica_groups=mesh['prow'=16,'pcol'=2] {'prow'}, dimensions={1}, use_global_device_ids=true | all-gather | bytes 278528 | tf_op jit(solution)/shard_map/all_gather | solution.py:51
  227.5 0.4 fusion.4
  227.9 3.4 psum.39
  231.3 1.0 convolution_multiply_fusion.4
  232.4 72.4 %all-gather.11.cloned.1.call-done = f32[512,8,256]{2,0,1:T(8,128)} async-done(((f32[32,8,256]{2,0,1:T(8,128)}), f32[512,8,256]{2,0,1:T(8,128)}) %all-gather.11.cloned.1.call-update) | async-done | bytes 4194320 | tf_op jit(solution)/shard_map/all_gather | solution.py:75
  304.8 2.5 reduce_sum.180
  307.3 1.8 all_gather.57
  309.2 1.0 convolution_multiply_fusion.3
  310.2 40.1 %all_gather.56 = bf16[32,16,256]{2,0,1:T(8,128)(2,1)S(1)} all-gather(bf16[32,1,256]{2,0,1:T(8,128)(2,1)S(1)} %get-tuple-element.12), channel_id=1, replica_groups=mesh['prow'=16,'pcol'=2] {'prow'}, dimensions={1}, use_global_device_ids=true | all-gather | bytes 278528 | tf_op jit(solution)/shard_map/all_gather | solution.py:51
  350.4 35.7 %all-gather.13.cloned.1.call-done = f32[512,8,256]{2,0,1:T(8,128)} async-done(((f32[32,8,256]{2,0,1:T(8,128)}), f32[512,8,256]{2,0,1:T(8,128)}) %all-gather.13.cloned.1.call-update) | async-done | bytes 4194320 | tf_op jit(solution)/shard_map/all_gather | solution.py:75
  386.1 2.5 reduce_sum.181
  388.7 1.8 all_gather.59
  390.5 1.0 convolution_multiply_fusion.2
  391.5 74.8 %all-gather.15.cloned.1.call-done = f32[512,8,256]{2,0,1:T(8,128)} async-done(((f32[32,8,256]{2,0,1:T(8,128)}), f32[512,8,256]{2,0,1:T(8,128)}) %all-gather.15.cloned.1.call-update) | async-done | bytes 4194320 | tf_op jit(solution)/shard_map/all_gather | solution.py:75
  466.4 2.5 reduce_sum.182
  468.9 1.8 all_gather.61
  470.7 1.0 convolution_multiply_fusion.1
  471.8 74.8 %all-gather.17.cloned.1.call-done = f32[512,8,256]{2,0,1:T(8,128)} async-done(((f32[32,8,256]{2,0,1:T(8,128)}), f32[512,8,256]{2,0,1:T(8,128)}) %all-gather.17.cloned.1.call-update) | async-done | bytes 4194320 | tf_op jit(solution)/shard_map/all_gather | solution.py:75
  546.6 2.5 reduce_sum.183
  549.1 1.8 all_gather.63
  551.0 1.0 convolution_multiply_fusion
  552.0 0.6 copy.80
  552.6 74.2 %all-gather.19.cloned.1.call-done = f32[512,8,256]{2,0,1:T(8,128)} async-done(((f32[32,8,256]{2,0,1:T(8,128)}), f32[512,8,256]{2,0,1:T(8,128)}) %all-gather.19.cloned.1.call-update) | async-done | bytes 4194320 | tf_op jit(solution)/shard_map/all_gather | solution.py:75
  626.8 2.5 reduce_sum.184
  629.4 0.9 copy.81
  (34 shorter events, 1.0 us)
Async XLA Ops:
  7.2 52.5 %copy-start = (bf16[1,256,8,256]{3,2,1,0:T(8,128)(2,1)S(1)}, bf16[1,256,8,256]{3,2,1,0:T(8,128)(2,1)}, u32[]{:S(2)}) copy-start(bf16[1,256,8,256]{3,2,1,0:T(8,128)(2,1)} %param.5) | copy-start | bytes 3145732
  7.2 181.3 %copy-start.1 = (f32[32,1,256]{2,1,0:T(1,128)S(1)}, f32[32,1,256]{2,1,0:T(1,128)}, u32[]{:S(2)}) copy-start(f32[32,1,256]{2,1,0:T(1,128)} %param.4) | copy-start | bytes 98308
  7.2 297.6 %all-gather.11.cloned.1.call-start = ((), (), s32[]{:S(2)}) async-start(), calls=%async_computation | async-start | bytes 4456448 | tf_op jit(solution)/shard_map/all_gather | solution.py:75
  232.3 153.8 %all-gather.13.cloned.1.call-start = ((), (), s32[]{:S(2)}) async-start(), calls=%async_computation.1 | async-start | bytes 4456448 | tf_op jit(solution)/shard_map/all_gather | solution.py:75
  310.2 156.2 %all-gather.15.cloned.1.call-start = ((), (), s32[]{:S(2)}) async-start(), calls=%async_computation.2 | async-start | bytes 4456448 | tf_op jit(solution)/shard_map/all_gather | solution.py:75
  391.5 155.1 %all-gather.17.cloned.1.call-start = ((), (), s32[]{:S(2)}) async-start(), calls=%async_computation.3 | async-start | bytes 4456448 | tf_op jit(solution)/shard_map/all_gather | solution.py:75
  471.7 155.1 %all-gather.19.cloned.1.call-start = ((), (), s32[]{:S(2)}) async-start(), calls=%async_computation.4 | async-start | bytes 4456448 | tf_op jit(solution)/shard_map/all_gather | solution.py:75
Sparse Core Ops, SparseCore 0:
  232.5 72.3 all-gather.10
  310.3 75.7 all-gather.12
  391.6 74.6 all-gather.14
  471.9 74.6 all-gather.16
  552.1 74.6 all-gather.18
